TPU v7x, 32 devices: a whole 2x2x4 slice. The times are simulated.
32 devices in a mesh: band: 4 (over x, core), lev: 8 (over z, y).
Axes of the slice: x: 2, y: 2, z: 4, core: 2. Of those that a mesh axis runs over, the one named last changes fastest.
Arguments:
- grid_in: bfloat16 [3, 32, 16, 2688], P(None, 'lev', 'band'), may hold values from -6 to 6
- row_shift: int32 [16], P('band'), may hold values from -3 to 0
- block_shift: int32 [16], P('band'), may hold values from 0 to 20
- interp_weights: bfloat16 [16, 4, 3, 128, 128], P('band'), may hold values from -0.15625 to 0.15625
- wave_order: int32 [128], replicated, may hold values from 0 to 127, as said below
- legendre: bfloat16 [128, 16, 1280], P('band'), may hold values from -1.5 to 1.5
Outputs:
- spectral: bfloat16 [3, 32, 128, 2, 1280], P(None, 'lev', 'band')
Inputs may be any that keep to these rules, and one draw needn't show every extreme that they name: `row_shift`: each latitude's stencil rows lie within 3 rows of it on both sides. `wave_order`: a permutation of the 128 wavenumbers; slots d * 32 to (d + 1) * 32 - 1 hold exactly one wavenumber of each aligned run of 4 consecutive wavenumbers.
All inputs are finite; a program needn't handle non-finite values.
Results may differ from a plain program's by a relative error of at most 0.0065.
Values may be sent and summed in bfloat16 or wider, within the bound.
A program may use at most 128 MiB of HBM per device.

v0:
```python
import math
import jax
import jax.numpy as jnp
from jax import lax
from jax.sharding import PartitionSpec as P

BLK = 128
HALO = 3
STENCIL = 4


def with_halo(block, sides, width):
    for axis, dim in sides:
        count = lax.axis_size(axis)
        forward = [(i, i + 1) for i in range(count - 1)]
        backward = [(target, source) for source, target in forward]
        low = lax.ppermute(
            lax.slice_in_dim(block, block.shape[dim] - width, None, axis=dim), axis, forward
        )
        high = lax.ppermute(lax.slice_in_dim(block, 0, width, axis=dim), axis, backward)
        block = jnp.concatenate([low, block, high], axis=dim)
    return block


def make_table(waves, longitudes):
    column = jnp.arange(longitudes, dtype=jnp.int32)[:, None]
    phase = column * waves[None, :] % longitudes
    angle = phase.astype(jnp.float32) * (2.0 * math.pi / longitudes)
    paired = jnp.stack([jnp.cos(angle), -jnp.sin(angle)], axis=2)
    return (paired.reshape(longitudes, 2 * waves.shape[0]) / math.sqrt(longitudes)).astype(
        jnp.bfloat16
    )


def stencil_rows(source, row_index, row_shift, block_shift):
    start = row_index + HALO + row_shift[row_index]
    rows = lax.dynamic_slice_in_dim(source, start, STENCIL, 2)
    rows = jnp.roll(rows, -block_shift[row_index] * BLK, axis=3)
    return rows.reshape(rows.shape[0], rows.shape[1], STENCIL, rows.shape[3] // BLK, BLK)


def vertical_terms(rows, weights, depth):
    total = None
    for level_step in range(3):
        term = jnp.einsum(
            "flsbj,sji->flbi",
            rows[:, level_step : level_step + depth],
            weights[:, level_step],
            preferred_element_type=jnp.float32,
        )
        total = term if total is None else total + term
    return total.reshape(total.shape[0], total.shape[1], total.shape[2] * total.shape[3])


def per_device(grid_in, row_shift, block_shift, interp_weights, wave_order, legendre):
    fields, depth, lat_rows, longitudes = grid_in.shape
    owned, latitudes, degrees = legendre.shape
    widened = with_halo(grid_in, (("band", 2),), HALO)
    extended = with_halo(widened, (("lev", 1),), 1)
    pieces = []
    for row_index in range(lat_rows):
        rows = stencil_rows(extended, row_index, row_shift, block_shift)
        pieces.append(vertical_terms(rows, interp_weights[row_index], depth))
    combined = jnp.stack(pieces, axis=2)
    interp = combined.astype(jnp.bfloat16)
    items = fields * depth
    own_waves = lax.dynamic_slice_in_dim(wave_order, lax.axis_index("band") * owned, owned)
    degree = jnp.arange(degrees, dtype=jnp.int32)[None, :]
    keep = degree >= own_waves[:, None]
    table = make_table(wave_order, longitudes)
    fourier = jnp.dot(
        interp.reshape(items * lat_rows, longitudes), table, preferred_element_type=jnp.float32
    )
    fourier = fourier.astype(jnp.bfloat16).reshape(items, lat_rows, table.shape[1])
    coeffs = lax.all_to_all(fourier, "band", split_axis=2, concat_axis=1, tiled=True)
    shaped = coeffs.reshape(coeffs.shape[0], latitudes, owned, 2)
    result = jnp.einsum("arqc,qrn->aqcn", shaped, legendre, preferred_element_type=jnp.float32)
    result = jnp.where(keep[None, :, None, :], result, jnp.zeros((), jnp.float32))
    spectral = result.astype(jnp.bfloat16)
    return spectral.reshape(fields, depth, owned, 2, degrees)


def solution(mesh):
    return jax.shard_map(
        per_device,
        mesh=mesh,
        in_specs=(
            P(None, "lev", "band", None),
            P("band"),
            P("band"),
            P("band", None, None, None, None),
            P(),
            P("band", None, None),
        ),
        out_specs=P(None, "lev", "band", None, None),
        check_vma=False,
    )
```

profile of v0, /device:TPU:8, one launch (start us, length us, event | category | flops | bytes accessed | tf_op | source)
XLA Modules:
  0.0 109.0 jit_solution(10730107957513051599)
XLA Ops:
  0.0 2.2 %fusion.27 = (bf16[3,4,3,2688]{3,2,1,0:T(4,128)(2,1)}, bf16[3,4,3,2688]{3,2,1,0:T(4,128)(2,1)}) fusion(bf16[3,4,4,2688]{3,2,1,0:T(4,128)(2,1)} %param.8), kind=kLoop, calls=%fused_computation.79 | loop fusion | bytes 774144 | tf_op jit(solution)/shard_map/slice | solution.py:18
  2.2 2.6 %collective-permute-start = (bf16[3,4,3,2688]{3,2,1,0:T(4,128)(2,1)}, bf16[3,4,3,2688]{3,2,1,0:T(4,128)(2,1)}, u32[]{:S(2)}, u32[]{:S(2)}) collective-permute-start(bf16[3,4,3,2688]{3,2,1,0:T(4,128)(2,1)} %get-tuple-element.16), channel_id=1, source_target_pairs={{0,8},{8,16},{16,24},{1,9},{9,17},{17,25},{2,10},{10,18},{18,26},{... | collective-permute-start | bytes 580616 | tf_op jit(solution)/shard_map/ppermute | solution.py:17
  4.8 1.3 %collective-permute-start.1 = (bf16[3,4,3,2688]{3,2,1,0:T(4,128)(2,1)}, bf16[3,4,3,2688]{3,2,1,0:T(4,128)(2,1)}, u32[]{:S(2)}, u32[]{:S(2)}) collective-permute-start(bf16[3,4,3,2688]{3,2,1,0:T(4,128)(2,1)} %get-tuple-element.17), channel_id=1, source_target_pairs={{8,0},{16,8},{24,16},{9,1},{17,9},{25,17},{10,2},{18,10},{26,18},{... | collective-permute-start | bytes 580616 | tf_op jit(solution)/shard_map/ppermute | solution.py:20
  6.1 1.5 %fusion.29 = (s32[1]{0:T(128)}, s32[1]{0:T(128)}, s32[1]{0:T(128)}, s32[1]{0:T(128)}) fusion(s32[4]{0:T(128)} %param.10), kind=kLoop, calls=%fused_computation.81 | loop fusion | bytes 32 | tf_op jit(solution)/shard_map/slice | solution.py:38
  10.2 7.3 %fusion.6 = (f32[2688,128,1]{1,0,2:T(8,128)S(1)}, f32[2688,128,1]{1,0,2:T(8,128)}) fusion(s32[128]{0:T(128)} %param.12), kind=kLoop, calls=%fused_computation.12 | loop fusion | flops 3440640 | bytes 2753024 | tf_op jit(solution)/shard_map/cos | solution.py:29
  17.6 0.7 fusion.28
  23.5 2.5 %fusion.26 = (bf16[1,4,3,128,128]{4,3,2,1,0:T(8,128)(2,1)}, bf16[1,4,3,128,128]{4,3,2,1,0:T(8,128)(2,1)S(1)}, bf16[1,4,3,128,128]{4,3,2,1,0:T(8,128)(2,1)}, bf16[1,4,3,128,128]{4,3,2,1,0:T(8,128)(2,1)}) fusion(bf16[4,4,3,128,128]{4,3,2,1,0:T(8,128)(2,1)} %param.11), kind=kLoop, calls=%fused_computation.78 | loop fusion | bytes 3145728 | tf_op jit(solution)/shard_map/slice | solution.py:63
  26.1 1.4 %fusion.1 = bf16[2688,128,2]{1,0,2:T(8,128)(2,1)} fusion(f32[2688,128,1]{1,0,2:T(8,128)S(1)} %copy-done.1, f32[2688,128,1]{1,0,2:T(8,128)S(1)} %get-tuple-element.18), kind=kLoop, calls=%fused_computation.3 | loop fusion | flops 2064384 | bytes 4128768 | tf_op jit(solution)/shard_map/convert_element_type | solution.py:30
  27.4 4.8 %copy.57 = bf16[2688,128,2]{0,2,1:T(2,128)(2,1)} copy(bf16[2688,128,2]{1,0,2:T(8,128)(2,1)} %fusion.1) | data formatting | bytes 2752512 | tf_op jit(solution)/shard_map/convert_element_type | solution.py:30
  32.2 3.3 %convert_element_type.49 = bf16[2688,256]{0,1:T(8,128)(2,1)S(1)} reshape(bf16[2688,128,2]{0,2,1:T(2,128)(2,1)} %copy.57) | data formatting | bytes 2752512 | tf_op jit(solution)/shard_map/convert_element_type | solution.py:30
  35.6 2.1 %copy_bitcast_fusion.2 = (bf16[4,3,128,128]{3,2,0,1:T(8,128)(2,1)}, bf16[4,3,128,128]{3,2,0,1:T(8,128)(2,1)}) fusion(bf16[1,4,3,128,128]{4,3,2,1,0:T(8,128)(2,1)} %get-tuple-element.8, bf16[1,4,3,128,128]{4,3,2,1,0:T(8,128)(2,1)} %get-tuple-element.6), kind=kLoop, calls=%fused_computation.50 | loop fusion | bytes 1572864 | tf_op jit(solution)/shard_map/squeeze | solution.py:63
  37.7 1.2 %pad_maximum_fusion.3 = (bf16[3,1,10,2688]{3,2,1,0:T(8,128)(2,1)S(1)}, bf16[3,1,10,2688]{3,2,1,0:T(8,128)(2,1)S(1)}) fusion(bf16[3,4,3,2688]{3,2,1,0:T(4,128)(2,1)} %collective-permute-done.1, bf16[3,4,4,2688]{3,2,1,0:T(4,128)(2,1)S(1)} %copy-done.4, bf16[3,4,3,2688]{3,2,1,0:T(4,128)(2,1)} %collective-permute-done), kind=kLoop, calls=%fused_computation.59 | loop fusion | flops 967680 | bytes 967680 | tf_op jit(solution)/shard_map/slice | solution.py:18
  38.9 3.4 %collective-permute-start.2 = (bf16[3,1,10,2688]{3,2,1,0:T(8,128)(2,1)S(1)}, bf16[3,1,10,2688]{3,2,1,0:T(8,128)(2,1)S(1)}, u32[]{:S(2)}, u32[]{:S(2)}) collective-permute-start(bf16[3,1,10,2688]{3,2,1,0:T(8,128)(2,1)S(1)} %get-tuple-element.14), channel_id=1, source_target_pairs={{0,1},{1,2},{2,3},{3,4},{4,5},{5,6},{6,7},{8,9},{9,10},{10,11},{11... | collective-permute-start | bytes 483848 | tf_op jit(solution)/shard_map/ppermute | solution.py:17
  42.4 3.5 %collective-permute-start.3 = (bf16[3,1,10,2688]{3,2,1,0:T(8,128)(2,1)S(1)}, bf16[3,1,10,2688]{3,2,1,0:T(8,128)(2,1)S(1)}, u32[]{:S(2)}, u32[]{:S(2)}) collective-permute-start(bf16[3,1,10,2688]{3,2,1,0:T(8,128)(2,1)S(1)} %get-tuple-element.15), channel_id=1, source_target_pairs={{1,0},{2,1},{3,2},{4,3},{5,4},{6,5},{7,6},{9,8},{10,9},{11,10},{12... | collective-permute-start | bytes 483848 | tf_op jit(solution)/shard_map/ppermute | solution.py:20
  45.9 1.0 copy_bitcast_fusion
  46.9 6.8 %collective-permute-done.2 = bf16[3,1,10,2688]{3,2,1,0:T(8,128)(2,1)S(1)} collective-permute-done((bf16[3,1,10,2688]{3,2,1,0:T(8,128)(2,1)S(1)}, bf16[3,1,10,2688]{3,2,1,0:T(8,128)(2,1)S(1)}, u32[]{:S(2)}, u32[]{:S(2)}) %collective-permute-start.2) | collective-permute-done | bytes 161312 | tf_op jit(solution)/shard_map/ppermute | solution.py:17
  53.7 2.7 %collective-permute-done.3 = bf16[3,1,10,2688]{3,2,1,0:T(8,128)(2,1)S(1)} collective-permute-done((bf16[3,1,10,2688]{3,2,1,0:T(8,128)(2,1)S(1)}, bf16[3,1,10,2688]{3,2,1,0:T(8,128)(2,1)S(1)}, u32[]{:S(2)}, u32[]{:S(2)}) %collective-permute-start.3) | collective-permute-done | bytes 161312 | tf_op jit(solution)/shard_map/ppermute | solution.py:20
  56.3 1.7 %pad_maximum_fusion = bf16[3,6,10,2688]{3,2,1,0:T(8,128)(2,1)S(1)} fusion(bf16[3,1,10,2688]{3,2,1,0:T(8,128)(2,1)S(1)} %collective-permute-done.3, bf16[3,4,3,2688]{3,2,1,0:T(4,128)(2,1)} %collective-permute-done.1, bf16[3,4,4,2688]{3,2,1,0:T(4,128)(2,1)S(1)} %copy-done.4, bf16[3,4,3,2688]{3,2,1,0:T(4,128)(2,1)} %collective-permute-done, ...), kind=kLoop, calls=%fused_computation.5 | loop fusion | flops 4838400 | bytes 1935360 | tf_op jit(solution)/shard_map/concatenate | solution.py:21
  58.0 1.9 %constant_dynamic-slice_fusion.3 = (bf16[3,6,4,2688]{3,2,1,0:T(4,128)(2,1)S(1)}, bf16[3,6,4,2688]{3,2,1,0:T(4,128)(2,1)}, bf16[3,6,4,2688]{3,2,1,0:T(4,128)(2,1)}, bf16[3,6,4,2688]{3,2,1,0:T(4,128)(2,1)S(1)}) fusion(bf16[3,6,10,2688]{3,2,1,0:T(8,128)(2,1)S(1)} %pad_maximum_fusion, s32[]{:T(128)S(6)} %select_n.48, s32[]{:T(128)S(6)} %select_n.51, ...), kind=kLoop, calls=%fused_computation.77 | loop fusion | bytes 3096592 | tf_op jit(solution)/shard_map/dynamic_slice | solution.py:37
  60.0 2.4 %fusion.23 = (bf16[3,6,4,2688]{3,2,1,0:T(4,128)(2,1)}, bf16[3,6,4,2688]{3,2,1,0:T(4,128)(2,1)}) fusion(s32[]{:T(128)S(6)} %select_n.63, bf16[3,6,4,2688]{3,2,1,0:T(4,128)(2,1)S(1)} %get-tuple-element.13, s32[]{:T(128)S(6)} %select_n.61, bf16[3,6,4,2688]{3,2,1,0:T(4,128)(2,1)S(1)} %get-tuple-element.10), kind=kLoop, calls=%fused_computation.54 | loop fusion | flops 1548288 | bytes 1548296 | tf_op jit(solution)/shard_map/jit(_roll_dynamic)/concatenate | solution.py:38
  62.4 1.2 %reshape.167 = bf16[3,6,4,21,128]{4,3,2,1,0:T(8,128)(2,1)S(1)} reshape(bf16[3,6,4,2688]{3,2,1,0:T(4,128)(2,1)} %get-tuple-element.30) | data formatting | bytes 774144 | tf_op jit(solution)/shard_map/reshape | solution.py:39
  63.6 1.9 %convolution_bitcast_fusion.6 = f32[3,4,21,128]{3,2,1,0:T(8,128)} fusion(bf16[3,6,4,21,128]{4,3,2,1,0:T(8,128)(2,1)S(1)} %reshape.167, bf16[4,3,128,128]{3,2,0,1:T(8,128)(2,1)} %get-tuple-element.34), kind=kOutput, calls=%fused_computation.21 | convolution fusion | flops 33030144 | bytes 647168 | tf_op jit(solution)/shard_map/flsbj,sji->flbi/dot_general | solution.py:45
  65.5 1.8 %convolution_bitcast_fusion.7 = f32[3,4,21,128]{3,2,1,0:T(8,128)} fusion(bf16[3,6,4,21,128]{4,3,2,1,0:T(8,128)(2,1)S(1)} %reshape.167, bf16[4,3,128,128]{3,2,0,1:T(8,128)(2,1)} %get-tuple-element.34), kind=kOutput, calls=%fused_computation.22 | convolution fusion | flops 33030144 | bytes 647168 | tf_op jit(solution)/shard_map/flsbj,sji->flbi/dot_general | solution.py:45
  67.4 1.1 %reshape.166 = bf16[3,6,4,21,128]{4,3,2,1,0:T(8,128)(2,1)S(1)} reshape(bf16[3,6,4,2688]{3,2,1,0:T(4,128)(2,1)} %get-tuple-element.31) | data formatting | bytes 774144 | tf_op jit(solution)/shard_map/reshape | solution.py:39
  68.5 0.9 convolution_bitcast_fusion.9
  69.4 0.9 convolution_bitcast_fusion.10
  70.4 2.4 %fusion.21 = (bf16[3,6,4,2688]{3,2,1,0:T(4,128)(2,1)}, bf16[3,6,4,2688]{3,2,1,0:T(4,128)(2,1)}) fusion(s32[]{:T(128)S(6)} %select_n.67, bf16[3,6,4,2688]{3,2,1,0:T(4,128)(2,1)S(1)} %copy-done.7, s32[]{:T(128)S(6)} %select_n.65, bf16[3,6,4,2688]{3,2,1,0:T(4,128)(2,1)S(1)} %copy-done.8), kind=kLoop, calls=%fused_computation.52 | loop fusion | flops 1548288 | bytes 1548296 | tf_op jit(solution)/shard_map/jit(_roll_dynamic)/concatenate | solution.py:38
  72.8 1.9 %reshape.169 = bf16[3,6,4,21,128]{4,3,2,1,0:T(8,128)(2,1)} reshape(bf16[3,6,4,2688]{3,2,1,0:T(4,128)(2,1)} %get-tuple-element.28) | data formatting | bytes 774144 | tf_op jit(solution)/shard_map/reshape | solution.py:39
  74.7 1.9 %convolution_bitcast_fusion = f32[3,4,21,128]{3,2,1,0:T(8,128)} fusion(bf16[3,6,4,21,128]{4,3,2,1,0:T(8,128)(2,1)} %reshape.169, bf16[4,3,128,128]{3,2,0,1:T(8,128)(2,1)} %get-tuple-element.32), kind=kOutput, calls=%fused_computation.15 | convolution fusion | flops 33030144 | bytes 702464 | tf_op jit(solution)/shard_map/flsbj,sji->flbi/dot_general | solution.py:45
  76.6 1.9 %convolution_bitcast_fusion.1 = f32[3,4,21,128]{3,2,1,0:T(8,128)} fusion(bf16[3,6,4,21,128]{4,3,2,1,0:T(8,128)(2,1)} %reshape.169, bf16[4,3,128,128]{3,2,0,1:T(8,128)(2,1)} %get-tuple-element.32), kind=kOutput, calls=%fused_computation.16 | convolution fusion | flops 33030144 | bytes 702464 | tf_op jit(solution)/shard_map/flsbj,sji->flbi/dot_general | solution.py:45
  78.5 1.9 %reshape.168 = bf16[3,6,4,21,128]{4,3,2,1,0:T(8,128)(2,1)} reshape(bf16[3,6,4,2688]{3,2,1,0:T(4,128)(2,1)} %get-tuple-element.29) | data formatting | bytes 774144 | tf_op jit(solution)/shard_map/reshape | solution.py:39
  80.4 1.9 %convolution_bitcast_fusion.3 = f32[3,4,21,128]{3,2,1,0:T(8,128)} fusion(bf16[3,6,4,21,128]{4,3,2,1,0:T(8,128)(2,1)} %reshape.168, bf16[4,3,128,128]{3,2,0,1:T(8,128)(2,1)} %get-tuple-element.33), kind=kOutput, calls=%fused_computation.18 | convolution fusion | flops 33030144 | bytes 702464 | tf_op jit(solution)/shard_map/flsbj,sji->flbi/dot_general | solution.py:45
  82.3 1.9 %convolution_bitcast_fusion.4 = f32[3,4,21,128]{3,2,1,0:T(8,128)} fusion(bf16[3,6,4,21,128]{4,3,2,1,0:T(8,128)(2,1)} %reshape.168, bf16[4,3,128,128]{3,2,0,1:T(8,128)(2,1)} %get-tuple-element.33), kind=kOutput, calls=%fused_computation.19 | convolution fusion | flops 33030144 | bytes 702464 | tf_op jit(solution)/shard_map/flsbj,sji->flbi/dot_general | solution.py:45
  84.2 1.9 %fusion.19 = bf16[3,4,21,128]{3,2,1,0:T(8,128)(2,1)} fusion(f32[3,4,21,128]{3,2,1,0:T(8,128)} %convolution_bitcast_fusion.6, f32[3,4,21,128]{3,2,1,0:T(8,128)} %convolution_bitcast_fusion.7, bf16[3,6,4,21,128]{4,3,2,1,0:T(8,128)(2,1)S(1)} %copy-done.3, bf16[4,3,128,128]{3,2,0,1:T(8,128)(2,1)} %get-tuple-element.34), kind=kOutput, calls=%fused_computation.37 | convolution fusion | flops 33126912 | bytes 877568 | tf_op jit(solution)/shard_map/flsbj,sji->flbi/dot_general | solution.py:45
  86.1 1.6 %stack_reshape.17 = bf16[3,4,1,2688]{3,1,0,2:T(4,128)(2,1)} reshape(bf16[3,4,21,128]{3,2,1,0:T(8,128)(2,1)} %fusion.19) | data formatting | bytes 129024 | tf_op jit(solution)/shard_map/stack;reshape | solution.py:64
  87.7 1.9 %fusion.20 = bf16[3,4,21,128]{3,2,1,0:T(8,128)(2,1)} fusion(f32[3,4,21,128]{3,2,1,0:T(8,128)} %convolution_bitcast_fusion.9, f32[3,4,21,128]{3,2,1,0:T(8,128)} %convolution_bitcast_fusion.10, bf16[3,6,4,21,128]{4,3,2,1,0:T(8,128)(2,1)S(1)} %reshape.166, bf16[4,3,128,128]{3,2,0,1:T(8,128)(2,1)S(1)} %copy-done.6), kind=kOutput, calls=%fused_computation.38 | convolution fusion | flops 33126912 | bytes 896000 | tf_op jit(solution)/shard_map/flsbj,sji->flbi/dot_general | solution.py:45
  89.5 0.9 stack_reshape.16
  90.5 1.4 %fusion.17 = bf16[3,4,21,128]{3,2,1,0:T(8,128)(2,1)S(1)} fusion(f32[3,4,21,128]{3,2,1,0:T(8,128)} %convolution_bitcast_fusion, f32[3,4,21,128]{3,2,1,0:T(8,128)} %convolution_bitcast_fusion.1, bf16[3,6,4,21,128]{4,3,2,1,0:T(8,128)(2,1)} %reshape.169, bf16[4,3,128,128]{3,2,0,1:T(8,128)(2,1)} %get-tuple-element.32), kind=kOutput, calls=%fused_computation.35 | convolution fusion | flops 33126912 | bytes 932864 | tf_op jit(solution)/shard_map/flsbj,sji->flbi/dot_general | solution.py:45
  91.9 1.4 %fusion.18 = bf16[3,4,21,128]{3,2,1,0:T(8,128)(2,1)S(1)} fusion(f32[3,4,21,128]{3,2,1,0:T(8,128)} %convolution_bitcast_fusion.3, f32[3,4,21,128]{3,2,1,0:T(8,128)} %convolution_bitcast_fusion.4, bf16[3,6,4,21,128]{4,3,2,1,0:T(8,128)(2,1)} %reshape.168, bf16[4,3,128,128]{3,2,0,1:T(8,128)(2,1)} %get-tuple-element.33), kind=kOutput, calls=%fused_computation.36 | convolution fusion | flops 33126912 | bytes 932864 | tf_op jit(solution)/shard_map/flsbj,sji->flbi/dot_general | solution.py:45
  93.4 0.2 pad_maximum_fusion.4
  93.8 0.5 convolution_convert_fusion
  94.6 1.0 reshape.198
  95.6 3.5 %all-to-all-start = ((bf16[4,2,1536]{2,1,0:T(2,128)(2,1)}), bf16[4,2,1536]{2,1,0:T(2,128)(2,1)S(1)}, u32[]{:S(2)}, u32[]{:S(2)}) async-start(bf16[4,2,1536]{2,1,0:T(2,128)(2,1)} %reshape.198), calls=%async_computation | async-start | bytes 49152 | tf_op jit(solution)/shard_map/all_to_all | solution.py:75
  99.2 3.6 %all-to-all-done = bf16[4,2,1536]{2,1,0:T(2,128)(2,1)S(1)} async-done(((bf16[4,2,1536]{2,1,0:T(2,128)(2,1)}), bf16[4,2,1536]{2,1,0:T(2,128)(2,1)S(1)}, u32[]{:S(2)}, u32[]{:S(2)}) %all-to-all-start) | async-done | bytes 24608 | tf_op jit(solution)/shard_map/all_to_all | solution.py:75
  102.8 0.6 reshape.199
  103.5 1.1 %fusion = bf16[12,32,2,1280]{3,0,2,1:T(8,128)(2,1)S(1)} fusion(pred[32,1280]{1,0:T(8,128)(4,1)S(1)} %iota_compare_fusion, bf16[32,16,1280]{2,1,0:T(8,128)(2,1)S(1)} %copy-done, bf16[12,16,32,2]{0,3,2,1:T(2,128)(2,1)S(1)} %bitcast.196), kind=kOutput, calls=%fused_computation.1 | convolution fusion | flops 33423360 | bytes 3342336 | tf_op jit(solution)/shard_map/arqc,qrn->aqcn/dot_general | solution.py:77
  104.6 1.1 copy.62
  105.7 3.3 %copy.63 = bf16[3,4,32,2,1280]{4,3,2,1,0:T(2,128)(2,1)} copy(bf16[3,4,32,2,1280]{4,2,3,1,0:T(8,128)(2,1)S(1)} %bitcast.195) | data formatting | bytes 3932160 | tf_op jit(solution)/shard_map/reshape | solution.py:80
  (35 shorter events, 0.8 us)
Async XLA Ops:
  0.0 103.5 %copy-start = (bf16[32,16,1280]{2,1,0:T(8,128)(2,1)S(1)}, bf16[32,16,1280]{2,1,0:T(8,128)(2,1)}, u32[]{:S(2)}) copy-start(bf16[32,16,1280]{2,1,0:T(8,128)(2,1)} %param.13) | copy-start | bytes 3932164
  2.2 15.3 %copy-start.11 = (s32[128]{0:T(128)S(1)}, s32[128]{0:T(128)}, u32[]{:S(2)}) copy-start(s32[128]{0:T(128)} %param.12) | copy-start | bytes 1540
  2.2 15.4 %copy-start.10 = (s32[4]{0:T(128)S(1)}, s32[4]{0:T(128)}, u32[]{:S(2)}) copy-start(s32[4]{0:T(128)} %param.9) | copy-start | bytes 52
  2.2 35.5 %collective-permute-start = (bf16[3,4,3,2688]{3,2,1,0:T(4,128)(2,1)}, bf16[3,4,3,2688]{3,2,1,0:T(4,128)(2,1)}, u32[]{:S(2)}, u32[]{:S(2)}) collective-permute-start(bf16[3,4,3,2688]{3,2,1,0:T(4,128)(2,1)} %get-tuple-element.16), channel_id=1, source_target_pairs={{0,8},{8,16},{16,24},{1,9},{9,17},{17,25},{2,10},{10,18},{18,26},{... | collective-permute-start | bytes 580616 | tf_op jit(solution)/shard_map/ppermute | solution.py:17
  4.8 32.9 %collective-permute-start.1 = (bf16[3,4,3,2688]{3,2,1,0:T(4,128)(2,1)}, bf16[3,4,3,2688]{3,2,1,0:T(4,128)(2,1)}, u32[]{:S(2)}, u32[]{:S(2)}) collective-permute-start(bf16[3,4,3,2688]{3,2,1,0:T(4,128)(2,1)} %get-tuple-element.17), channel_id=1, source_target_pairs={{8,0},{16,8},{24,16},{9,1},{17,9},{25,17},{10,2},{18,10},{26,18},{... | collective-permute-start | bytes 580616 | tf_op jit(solution)/shard_map/ppermute | solution.py:20
  23.5 2.5 %copy-start.1 = (f32[2688,128,1]{1,0,2:T(8,128)S(1)}, f32[2688,128,1]{1,0,2:T(8,128)}, u32[]{:S(2)}) copy-start(f32[2688,128,1]{1,0,2:T(8,128)} %get-tuple-element.19) | copy-start | bytes 4128772
  32.2 5.5 %copy-start.4 = (bf16[3,4,4,2688]{3,2,1,0:T(4,128)(2,1)S(1)}, bf16[3,4,4,2688]{3,2,1,0:T(4,128)(2,1)}, u32[]{:S(2)}) copy-start(bf16[3,4,4,2688]{3,2,1,0:T(4,128)(2,1)} %param.8) | copy-start | bytes 774148
  35.6 10.3 %copy-start.5 = (bf16[1,4,3,128,128]{4,3,2,1,0:T(8,128)(2,1)S(1)}, bf16[1,4,3,128,128]{4,3,2,1,0:T(8,128)(2,1)}, u32[]{:S(2)}) copy-start(bf16[1,4,3,128,128]{4,3,2,1,0:T(8,128)(2,1)} %get-tuple-element.9) | copy-start | bytes 1179652
  38.9 14.7 %collective-permute-start.2 = (bf16[3,1,10,2688]{3,2,1,0:T(8,128)(2,1)S(1)}, bf16[3,1,10,2688]{3,2,1,0:T(8,128)(2,1)S(1)}, u32[]{:S(2)}, u32[]{:S(2)}) collective-permute-start(bf16[3,1,10,2688]{3,2,1,0:T(8,128)(2,1)S(1)} %get-tuple-element.14), channel_id=1, source_target_pairs={{0,1},{1,2},{2,3},{3,4},{4,5},{5,6},{6,7},{8,9},{9,10},{10,11},{11... | collective-permute-start | bytes 483848 | tf_op jit(solution)/shard_map/ppermute | solution.py:17
  42.4 13.9 %collective-permute-start.3 = (bf16[3,1,10,2688]{3,2,1,0:T(8,128)(2,1)S(1)}, bf16[3,1,10,2688]{3,2,1,0:T(8,128)(2,1)S(1)}, u32[]{:S(2)}, u32[]{:S(2)}) collective-permute-start(bf16[3,1,10,2688]{3,2,1,0:T(8,128)(2,1)S(1)} %get-tuple-element.15), channel_id=1, source_target_pairs={{1,0},{2,1},{3,2},{4,3},{5,4},{6,5},{7,6},{9,8},{10,9},{11,10},{12... | collective-permute-start | bytes 483848 | tf_op jit(solution)/shard_map/ppermute | solution.py:20
  62.4 6.1 %copy-start.6 = (bf16[4,3,128,128]{3,2,0,1:T(8,128)(2,1)S(1)}, bf16[4,3,128,128]{3,2,0,1:T(8,128)(2,1)}, u32[]{:S(2)}) copy-start(bf16[4,3,128,128]{3,2,0,1:T(8,128)(2,1)} %get-tuple-element.35) | copy-start | bytes 1179652
  63.6 3.8 %copy-start.2 = (bf16[3,6,4,21,128]{4,3,2,1,0:T(8,128)(2,1)}, bf16[3,6,4,21,128]{4,3,2,1,0:T(8,128)(2,1)S(1)}, u32[]{:S(2)}) copy-start(bf16[3,6,4,21,128]{4,3,2,1,0:T(8,128)(2,1)S(1)} %reshape.167) | copy-start | bytes 1161220
  68.5 1.8 %copy-start.7 = (bf16[3,6,4,2688]{3,2,1,0:T(4,128)(2,1)S(1)}, bf16[3,6,4,2688]{3,2,1,0:T(4,128)(2,1)}, u32[]{:S(2)}) copy-start(bf16[3,6,4,2688]{3,2,1,0:T(4,128)(2,1)} %get-tuple-element.11) | copy-start | bytes 1161220
  68.5 1.8 %copy-start.8 = (bf16[3,6,4,2688]{3,2,1,0:T(4,128)(2,1)S(1)}, bf16[3,6,4,2688]{3,2,1,0:T(4,128)(2,1)}, u32[]{:S(2)}) copy-start(bf16[3,6,4,2688]{3,2,1,0:T(4,128)(2,1)} %get-tuple-element.12) | copy-start | bytes 1161220
  80.4 3.8 %copy-start.3 = (bf16[3,6,4,21,128]{4,3,2,1,0:T(8,128)(2,1)S(1)}, bf16[3,6,4,21,128]{4,3,2,1,0:T(8,128)(2,1)}, u32[]{:S(2)}) copy-start(bf16[3,6,4,21,128]{4,3,2,1,0:T(8,128)(2,1)} %copy-done.2) | copy-start | bytes 1161220
  89.5 3.8 %copy-start.9 = (bf16[3,4,1,2688]{3,1,0,2:T(4,128)(2,1)S(1)}, bf16[3,4,1,2688]{3,1,0,2:T(4,128)(2,1)}, u32[]{:S(2)}) copy-start(bf16[3,4,1,2688]{3,1,0,2:T(4,128)(2,1)} %stack_reshape.17) | copy-start | bytes 193540
  95.6 7.2 %all-to-all-start = ((bf16[4,2,1536]{2,1,0:T(2,128)(2,1)}), bf16[4,2,1536]{2,1,0:T(2,128)(2,1)S(1)}, u32[]{:S(2)}, u32[]{:S(2)}) async-start(bf16[4,2,1536]{2,1,0:T(2,128)(2,1)} %reshape.198), calls=%async_computation | async-start | bytes 49152 | tf_op jit(solution)/shard_map/all_to_all | solution.py:75
where the time goes:
time: 110 us; the launch traced here: 109 us
  local copies, waits for them, and re-layouts  35.3 us (32%)
  matrix products  21.3 us (19%)
  other arithmetic  16.8 us (15%)
  starting transfers between devices  14.3 us (13%)
  waiting for transfers between devices  13 us (12%)
  between operations  8.25 us (8%)
    dot_general x12, matrix products, vertical_terms(): jnp.einsum('flsbj,sji->flbi', rows[:, level_step:level_step + depth], wei...  19.7 us
    convert_element_type x2, local copies, waits for them, and re-layouts, make_table(): (paired.reshape(longitudes, 2 * waves.shape[0]) / math.sqrt(longitudes))....  8.07 us
    cos x1, other arithmetic, make_table(): paired = jnp.stack([jnp.cos(angle), -jnp.sin(angle)], axis=2)  7.3 us
    ppermute x2, waiting for transfers between devices, with_halo(): lax.ppermute(lax.slice_in_dim(block, block.shape[dim] - width, None, axis...  6.76 us
    reshape x4, local copies, waits for them, and re-layouts, stencil_rows(): rows.reshape(rows.shape[0], rows.shape[1], STENCIL, rows.shape[3] // BLK,...  6.17 us
    ppermute x2, starting transfers between devices, with_halo(): lax.ppermute(lax.slice_in_dim(block, block.shape[dim] - width, None, axis...  6 us
    concatenate x2, other arithmetic, stencil_rows(): rows = jnp.roll(rows, -block_shift[row_index] * BLK, axis=3)  4.86 us
    ppermute x2, starting transfers between devices, with_halo(): lax.ppermute(lax.slice_in_dim(block, 0, width, axis=dim), axis, backward)  4.77 us
  transfers between devices with their start and end apart: 5, of which 3 were waited for; matrix products, arithmetic and copies ran while one was open for 23% of the time, Pallas kernels for 0%

commit v1 on v0

--- a/solution.py
+++ b/solution.py
@@ -7,6 +7,12 @@
 BLK = 128
 HALO = 3
 STENCIL = 4
+
+
+def answer_domain_over_axis(packet, link_axis):
+    val2 = jnp.stack(jnp.split(packet, lax.axis_size(link_axis), axis=2))
+    state_next = lax.all_to_all(val2, link_axis, 0, 0)
+    return jnp.concatenate(state_next, axis=1)
 
 
 def with_halo(block, sides, width):
@@ -72,7 +78,7 @@
         interp.reshape(items * lat_rows, longitudes), table, preferred_element_type=jnp.float32
     )
     fourier = fourier.astype(jnp.bfloat16).reshape(items, lat_rows, table.shape[1])
-    coeffs = lax.all_to_all(fourier, "band", split_axis=2, concat_axis=1, tiled=True)
+    coeffs = answer_domain_over_axis(fourier, "band")
     shaped = coeffs.reshape(coeffs.shape[0], latitudes, owned, 2)
     result = jnp.einsum("arqc,qrn->aqcn", shaped, legendre, preferred_element_type=jnp.float32)
     result = jnp.where(keep[None, :, None, :], result, jnp.zeros((), jnp.float32))

time: 110 us -> 109 us (level)
  no operation moved by 1% of the time
where the time goes in v1:
time: 109 us; the launch traced here: 108 us
  local copies, waits for them, and re-layouts  34.5 us (32%)
  matrix products  21.3 us (20%)
  other arithmetic  16.8 us (15%)
  starting transfers between devices  14.3 us (13%)
  waiting for transfers between devices  13.1 us (12%)
  between operations  8 us (7%)
    dot_general x12, matrix products, vertical_terms(): jnp.einsum('flsbj,sji->flbi', rows[:, level_step:level_step + depth], wei...  19.7 us
    convert_element_type x2, local copies, waits for them, and re-layouts, make_table(): (paired.reshape(longitudes, 2 * waves.shape[0]) / math.sqrt(longitudes))....  8.06 us
    cos x1, other arithmetic, make_table(): paired = jnp.stack([jnp.cos(angle), -jnp.sin(angle)], axis=2)  7.3 us
    ppermute x2, waiting for transfers between devices, with_halo(): lax.ppermute(lax.slice_in_dim(block, block.shape[dim] - width, None, axis...  6.77 us
    reshape x4, local copies, waits for them, and re-layouts, stencil_rows(): rows.reshape(rows.shape[0], rows.shape[1], STENCIL, rows.shape[3] // BLK,...  6.16 us
    ppermute x2, starting transfers between devices, with_halo(): lax.ppermute(lax.slice_in_dim(block, block.shape[dim] - width, None, axis...  6 us
    concatenate x2, other arithmetic, stencil_rows(): rows = jnp.roll(rows, -block_shift[row_index] * BLK, axis=3)  4.81 us
    ppermute x2, starting transfers between devices, with_halo(): lax.ppermute(lax.slice_in_dim(block, 0, width, axis=dim), axis, backward)  4.77 us
  transfers between devices with their start and end apart: 5, of which 3 were waited for; matrix products, arithmetic and copies ran while one was open for 23% of the time, Pallas kernels for 0%

profile of v1, /device:TPU:8, one launch (start us, length us, event | category | flops | bytes accessed | tf_op | source)
XLA Modules:
  0.0 107.9 jit_solution(9838268111448065872)
XLA Ops:
  0.0 2.2 %fusion.27 = (bf16[3,4,3,2688]{3,2,1,0:T(4,128)(2,1)}, bf16[3,4,3,2688]{3,2,1,0:T(4,128)(2,1)}) fusion(bf16[3,4,4,2688]{3,2,1,0:T(4,128)(2,1)} %param.8), kind=kLoop, calls=%fused_computation.84 | loop fusion | bytes 774144 | tf_op jit(solution)/shard_map/slice | solution.py:24
  2.2 2.6 %collective-permute-start = (bf16[3,4,3,2688]{3,2,1,0:T(4,128)(2,1)}, bf16[3,4,3,2688]{3,2,1,0:T(4,128)(2,1)}, u32[]{:S(2)}, u32[]{:S(2)}) collective-permute-start(bf16[3,4,3,2688]{3,2,1,0:T(4,128)(2,1)} %get-tuple-element.16), channel_id=1, source_target_pairs={{0,8},{8,16},{16,24},{1,9},{9,17},{17,25},{2,10},{10,18},{18,26},{... | collective-permute-start | bytes 580616 | tf_op jit(solution)/shard_map/ppermute | solution.py:23
  4.8 1.3 %collective-permute-start.1 = (bf16[3,4,3,2688]{3,2,1,0:T(4,128)(2,1)}, bf16[3,4,3,2688]{3,2,1,0:T(4,128)(2,1)}, u32[]{:S(2)}, u32[]{:S(2)}) collective-permute-start(bf16[3,4,3,2688]{3,2,1,0:T(4,128)(2,1)} %get-tuple-element.17), channel_id=1, source_target_pairs={{8,0},{16,8},{24,16},{9,1},{17,9},{25,17},{10,2},{18,10},{26,18},{... | collective-permute-start | bytes 580616 | tf_op jit(solution)/shard_map/ppermute | solution.py:26
  6.1 1.5 %fusion.29 = (s32[1]{0:T(128)}, s32[1]{0:T(128)}, s32[1]{0:T(128)}, s32[1]{0:T(128)}) fusion(s32[4]{0:T(128)} %param.10), kind=kLoop, calls=%fused_computation.86 | loop fusion | bytes 32 | tf_op jit(solution)/shard_map/slice | solution.py:44
  10.2 7.3 %fusion.6 = (f32[2688,128,1]{1,0,2:T(8,128)S(1)}, f32[2688,128,1]{1,0,2:T(8,128)}) fusion(s32[128]{0:T(128)} %param.12), kind=kLoop, calls=%fused_computation.12 | loop fusion | flops 3440640 | bytes 2753024 | tf_op jit(solution)/shard_map/cos | solution.py:35
  17.6 0.7 fusion.28
  23.3 2.5 %fusion.26 = (bf16[1,4,3,128,128]{4,3,2,1,0:T(8,128)(2,1)}, bf16[1,4,3,128,128]{4,3,2,1,0:T(8,128)(2,1)S(1)}, bf16[1,4,3,128,128]{4,3,2,1,0:T(8,128)(2,1)}, bf16[1,4,3,128,128]{4,3,2,1,0:T(8,128)(2,1)}) fusion(bf16[4,4,3,128,128]{4,3,2,1,0:T(8,128)(2,1)} %param.11), kind=kLoop, calls=%fused_computation.83 | loop fusion | bytes 3145728 | tf_op jit(solution)/shard_map/slice | solution.py:69
  25.8 1.4 %fusion.1 = bf16[2688,128,2]{1,0,2:T(8,128)(2,1)} fusion(f32[2688,128,1]{1,0,2:T(8,128)S(1)} %copy-done.1, f32[2688,128,1]{1,0,2:T(8,128)S(1)} %get-tuple-element.22), kind=kLoop, calls=%fused_computation.3 | loop fusion | flops 2064384 | bytes 4128768 | tf_op jit(solution)/shard_map/convert_element_type | solution.py:36
  27.2 4.8 %copy.39 = bf16[2688,128,2]{0,2,1:T(2,128)(2,1)} copy(bf16[2688,128,2]{1,0,2:T(8,128)(2,1)} %fusion.1) | data formatting | bytes 2752512 | tf_op jit(solution)/shard_map/convert_element_type | solution.py:36
  32.0 3.3 %convert_element_type.49 = bf16[2688,256]{0,1:T(8,128)(2,1)S(1)} reshape(bf16[2688,128,2]{0,2,1:T(2,128)(2,1)} %copy.39) | data formatting | bytes 2752512 | tf_op jit(solution)/shard_map/convert_element_type | solution.py:36
  35.3 2.1 %copy_bitcast_fusion.2 = (bf16[4,3,128,128]{3,2,0,1:T(8,128)(2,1)}, bf16[4,3,128,128]{3,2,0,1:T(8,128)(2,1)}) fusion(bf16[1,4,3,128,128]{4,3,2,1,0:T(8,128)(2,1)} %get-tuple-element.8, bf16[1,4,3,128,128]{4,3,2,1,0:T(8,128)(2,1)} %get-tuple-element.6), kind=kLoop, calls=%fused_computation.50 | loop fusion | bytes 1572864 | tf_op jit(solution)/shard_map/squeeze | solution.py:69
  37.5 1.2 %pad_maximum_fusion.3 = (bf16[3,1,10,2688]{3,2,1,0:T(8,128)(2,1)S(1)}, bf16[3,1,10,2688]{3,2,1,0:T(8,128)(2,1)S(1)}) fusion(bf16[3,4,3,2688]{3,2,1,0:T(4,128)(2,1)} %collective-permute-done.1, bf16[3,4,4,2688]{3,2,1,0:T(4,128)(2,1)S(1)} %copy-done.4, bf16[3,4,3,2688]{3,2,1,0:T(4,128)(2,1)} %collective-permute-done), kind=kLoop, calls=%fused_computation.59 | loop fusion | flops 967680 | bytes 967680 | tf_op jit(solution)/shard_map/slice | solution.py:24
  38.7 3.4 %collective-permute-start.2 = (bf16[3,1,10,2688]{3,2,1,0:T(8,128)(2,1)S(1)}, bf16[3,1,10,2688]{3,2,1,0:T(8,128)(2,1)S(1)}, u32[]{:S(2)}, u32[]{:S(2)}) collective-permute-start(bf16[3,1,10,2688]{3,2,1,0:T(8,128)(2,1)S(1)} %get-tuple-element.14), channel_id=1, source_target_pairs={{0,1},{1,2},{2,3},{3,4},{4,5},{5,6},{6,7},{8,9},{9,10},{10,11},{11... | collective-permute-start | bytes 483848 | tf_op jit(solution)/shard_map/ppermute | solution.py:23
  42.1 3.5 %collective-permute-start.3 = (bf16[3,1,10,2688]{3,2,1,0:T(8,128)(2,1)S(1)}, bf16[3,1,10,2688]{3,2,1,0:T(8,128)(2,1)S(1)}, u32[]{:S(2)}, u32[]{:S(2)}) collective-permute-start(bf16[3,1,10,2688]{3,2,1,0:T(8,128)(2,1)S(1)} %get-tuple-element.15), channel_id=1, source_target_pairs={{1,0},{2,1},{3,2},{4,3},{5,4},{6,5},{7,6},{9,8},{10,9},{11,10},{12... | collective-permute-start | bytes 483848 | tf_op jit(solution)/shard_map/ppermute | solution.py:26
  45.7 1.0 copy_bitcast_fusion
  46.6 6.8 %collective-permute-done.2 = bf16[3,1,10,2688]{3,2,1,0:T(8,128)(2,1)S(1)} collective-permute-done((bf16[3,1,10,2688]{3,2,1,0:T(8,128)(2,1)S(1)}, bf16[3,1,10,2688]{3,2,1,0:T(8,128)(2,1)S(1)}, u32[]{:S(2)}, u32[]{:S(2)}) %collective-permute-start.2) | collective-permute-done | bytes 161312 | tf_op jit(solution)/shard_map/ppermute | solution.py:23
  53.4 2.7 %collective-permute-done.3 = bf16[3,1,10,2688]{3,2,1,0:T(8,128)(2,1)S(1)} collective-permute-done((bf16[3,1,10,2688]{3,2,1,0:T(8,128)(2,1)S(1)}, bf16[3,1,10,2688]{3,2,1,0:T(8,128)(2,1)S(1)}, u32[]{:S(2)}, u32[]{:S(2)}) %collective-permute-start.3) | collective-permute-done | bytes 161312 | tf_op jit(solution)/shard_map/ppermute | solution.py:26
  56.1 1.7 %pad_maximum_fusion = bf16[3,6,10,2688]{3,2,1,0:T(8,128)(2,1)S(1)} fusion(bf16[3,1,10,2688]{3,2,1,0:T(8,128)(2,1)S(1)} %collective-permute-done.3, bf16[3,4,3,2688]{3,2,1,0:T(4,128)(2,1)} %collective-permute-done.1, bf16[3,4,4,2688]{3,2,1,0:T(4,128)(2,1)S(1)} %copy-done.4, bf16[3,4,3,2688]{3,2,1,0:T(4,128)(2,1)} %collective-permute-done, ...), kind=kLoop, calls=%fused_computation.5 | loop fusion | flops 4838400 | bytes 1935360 | tf_op jit(solution)/shard_map/concatenate | solution.py:27
  57.8 1.9 %constant_dynamic-slice_fusion.3 = (bf16[3,6,4,2688]{3,2,1,0:T(4,128)(2,1)S(1)}, bf16[3,6,4,2688]{3,2,1,0:T(4,128)(2,1)}, bf16[3,6,4,2688]{3,2,1,0:T(4,128)(2,1)}, bf16[3,6,4,2688]{3,2,1,0:T(4,128)(2,1)S(1)}) fusion(bf16[3,6,10,2688]{3,2,1,0:T(8,128)(2,1)S(1)} %pad_maximum_fusion, s32[]{:T(128)S(6)} %select_n.48, s32[]{:T(128)S(6)} %select_n.51, ...), kind=kLoop, calls=%fused_computation.82 | loop fusion | bytes 3096592 | tf_op jit(solution)/shard_map/dynamic_slice | solution.py:43
  59.7 2.4 %fusion.23 = (bf16[3,6,4,2688]{3,2,1,0:T(4,128)(2,1)}, bf16[3,6,4,2688]{3,2,1,0:T(4,128)(2,1)}) fusion(s32[]{:T(128)S(6)} %select_n.63, bf16[3,6,4,2688]{3,2,1,0:T(4,128)(2,1)S(1)} %get-tuple-element.13, s32[]{:T(128)S(6)} %select_n.61, bf16[3,6,4,2688]{3,2,1,0:T(4,128)(2,1)S(1)} %get-tuple-element.10), kind=kLoop, calls=%fused_computation.54 | loop fusion | flops 1548288 | bytes 1548296 | tf_op jit(solution)/shard_map/jit(_roll_dynamic)/concatenate | solution.py:44
  62.1 1.2 %reshape.166 = bf16[3,6,4,21,128]{4,3,2,1,0:T(8,128)(2,1)S(1)} reshape(bf16[3,6,4,2688]{3,2,1,0:T(4,128)(2,1)} %get-tuple-element.34) | data formatting | bytes 774144 | tf_op jit(solution)/shard_map/reshape | solution.py:45
  63.3 1.9 %convolution_bitcast_fusion.6 = f32[3,4,21,128]{3,2,1,0:T(8,128)} fusion(bf16[3,6,4,21,128]{4,3,2,1,0:T(8,128)(2,1)S(1)} %reshape.166, bf16[4,3,128,128]{3,2,0,1:T(8,128)(2,1)} %get-tuple-element.38), kind=kOutput, calls=%fused_computation.21 | convolution fusion | flops 33030144 | bytes 647168 | tf_op jit(solution)/shard_map/flsbj,sji->flbi/dot_general | solution.py:51
  65.3 1.8 %convolution_bitcast_fusion.7 = f32[3,4,21,128]{3,2,1,0:T(8,128)} fusion(bf16[3,6,4,21,128]{4,3,2,1,0:T(8,128)(2,1)S(1)} %reshape.166, bf16[4,3,128,128]{3,2,0,1:T(8,128)(2,1)} %get-tuple-element.38), kind=kOutput, calls=%fused_computation.22 | convolution fusion | flops 33030144 | bytes 647168 | tf_op jit(solution)/shard_map/flsbj,sji->flbi/dot_general | solution.py:51
  67.1 1.1 %reshape.165 = bf16[3,6,4,21,128]{4,3,2,1,0:T(8,128)(2,1)S(1)} reshape(bf16[3,6,4,2688]{3,2,1,0:T(4,128)(2,1)} %get-tuple-element.35) | data formatting | bytes 774144 | tf_op jit(solution)/shard_map/reshape | solution.py:45
  68.2 0.9 convolution_bitcast_fusion.9
  69.1 0.9 convolution_bitcast_fusion.10
  70.1 2.4 %fusion.21 = (bf16[3,6,4,2688]{3,2,1,0:T(4,128)(2,1)}, bf16[3,6,4,2688]{3,2,1,0:T(4,128)(2,1)}) fusion(s32[]{:T(128)S(6)} %select_n.67, bf16[3,6,4,2688]{3,2,1,0:T(4,128)(2,1)S(1)} %copy-done.7, s32[]{:T(128)S(6)} %select_n.65, bf16[3,6,4,2688]{3,2,1,0:T(4,128)(2,1)S(1)} %copy-done.8), kind=kLoop, calls=%fused_computation.52 | loop fusion | flops 1548288 | bytes 1548296 | tf_op jit(solution)/shard_map/jit(_roll_dynamic)/concatenate | solution.py:44
  72.5 1.9 %reshape.168 = bf16[3,6,4,21,128]{4,3,2,1,0:T(8,128)(2,1)} reshape(bf16[3,6,4,2688]{3,2,1,0:T(4,128)(2,1)} %get-tuple-element.32) | data formatting | bytes 774144 | tf_op jit(solution)/shard_map/reshape | solution.py:45
  74.4 1.9 %convolution_bitcast_fusion = f32[3,4,21,128]{3,2,1,0:T(8,128)} fusion(bf16[3,6,4,21,128]{4,3,2,1,0:T(8,128)(2,1)} %reshape.168, bf16[4,3,128,128]{3,2,0,1:T(8,128)(2,1)} %get-tuple-element.36), kind=kOutput, calls=%fused_computation.15 | convolution fusion | flops 33030144 | bytes 702464 | tf_op jit(solution)/shard_map/flsbj,sji->flbi/dot_general | solution.py:51
  76.2 1.9 %convolution_bitcast_fusion.1 = f32[3,4,21,128]{3,2,1,0:T(8,128)} fusion(bf16[3,6,4,21,128]{4,3,2,1,0:T(8,128)(2,1)} %reshape.168, bf16[4,3,128,128]{3,2,0,1:T(8,128)(2,1)} %get-tuple-element.36), kind=kOutput, calls=%fused_computation.16 | convolution fusion | flops 33030144 | bytes 702464 | tf_op jit(solution)/shard_map/flsbj,sji->flbi/dot_general | solution.py:51
  78.2 1.9 %reshape.167 = bf16[3,6,4,21,128]{4,3,2,1,0:T(8,128)(2,1)} reshape(bf16[3,6,4,2688]{3,2,1,0:T(4,128)(2,1)} %get-tuple-element.33) | data formatting | bytes 774144 | tf_op jit(solution)/shard_map/reshape | solution.py:45
  80.1 1.9 %convolution_bitcast_fusion.3 = f32[3,4,21,128]{3,2,1,0:T(8,128)} fusion(bf16[3,6,4,21,128]{4,3,2,1,0:T(8,128)(2,1)} %reshape.167, bf16[4,3,128,128]{3,2,0,1:T(8,128)(2,1)} %get-tuple-element.37), kind=kOutput, calls=%fused_computation.18 | convolution fusion | flops 33030144 | bytes 702464 | tf_op jit(solution)/shard_map/flsbj,sji->flbi/dot_general | solution.py:51
  82.0 1.9 %convolution_bitcast_fusion.4 = f32[3,4,21,128]{3,2,1,0:T(8,128)} fusion(bf16[3,6,4,21,128]{4,3,2,1,0:T(8,128)(2,1)} %reshape.167, bf16[4,3,128,128]{3,2,0,1:T(8,128)(2,1)} %get-tuple-element.37), kind=kOutput, calls=%fused_computation.19 | convolution fusion | flops 33030144 | bytes 702464 | tf_op jit(solution)/shard_map/flsbj,sji->flbi/dot_general | solution.py:51
  83.9 1.9 %fusion.19 = bf16[3,4,21,128]{3,2,1,0:T(8,128)(2,1)} fusion(f32[3,4,21,128]{3,2,1,0:T(8,128)} %convolution_bitcast_fusion.6, f32[3,4,21,128]{3,2,1,0:T(8,128)} %convolution_bitcast_fusion.7, bf16[3,6,4,21,128]{4,3,2,1,0:T(8,128)(2,1)S(1)} %copy-done.3, bf16[4,3,128,128]{3,2,0,1:T(8,128)(2,1)} %get-tuple-element.38), kind=kOutput, calls=%fused_computation.37 | convolution fusion | flops 33126912 | bytes 877568 | tf_op jit(solution)/shard_map/flsbj,sji->flbi/dot_general | solution.py:51
  85.8 1.5 %stack_reshape.17 = bf16[3,4,1,2688]{3,1,0,2:T(4,128)(2,1)} reshape(bf16[3,4,21,128]{3,2,1,0:T(8,128)(2,1)} %fusion.19) | data formatting | bytes 129024 | tf_op jit(solution)/shard_map/stack;reshape | solution.py:70
  87.4 1.8 %fusion.20 = bf16[3,4,21,128]{3,2,1,0:T(8,128)(2,1)} fusion(f32[3,4,21,128]{3,2,1,0:T(8,128)} %convolution_bitcast_fusion.9, f32[3,4,21,128]{3,2,1,0:T(8,128)} %convolution_bitcast_fusion.10, bf16[3,6,4,21,128]{4,3,2,1,0:T(8,128)(2,1)S(1)} %reshape.165, bf16[4,3,128,128]{3,2,0,1:T(8,128)(2,1)S(1)} %copy-done.6), kind=kOutput, calls=%fused_computation.38 | convolution fusion | flops 33126912 | bytes 896000 | tf_op jit(solution)/shard_map/flsbj,sji->flbi/dot_general | solution.py:51
  89.2 0.9 stack_reshape.16
  90.1 1.4 %fusion.17 = bf16[3,4,21,128]{3,2,1,0:T(8,128)(2,1)S(1)} fusion(f32[3,4,21,128]{3,2,1,0:T(8,128)} %convolution_bitcast_fusion, f32[3,4,21,128]{3,2,1,0:T(8,128)} %convolution_bitcast_fusion.1, bf16[3,6,4,21,128]{4,3,2,1,0:T(8,128)(2,1)} %reshape.168, bf16[4,3,128,128]{3,2,0,1:T(8,128)(2,1)} %get-tuple-element.36), kind=kOutput, calls=%fused_computation.35 | convolution fusion | flops 33126912 | bytes 932864 | tf_op jit(solution)/shard_map/flsbj,sji->flbi/dot_general | solution.py:51
  91.6 1.4 %fusion.18 = bf16[3,4,21,128]{3,2,1,0:T(8,128)(2,1)S(1)} fusion(f32[3,4,21,128]{3,2,1,0:T(8,128)} %convolution_bitcast_fusion.3, f32[3,4,21,128]{3,2,1,0:T(8,128)} %convolution_bitcast_fusion.4, bf16[3,6,4,21,128]{4,3,2,1,0:T(8,128)(2,1)} %reshape.167, bf16[4,3,128,128]{3,2,0,1:T(8,128)(2,1)} %get-tuple-element.37), kind=kOutput, calls=%fused_computation.36 | convolution fusion | flops 33126912 | bytes 932864 | tf_op jit(solution)/shard_map/flsbj,sji->flbi/dot_general | solution.py:51
  93.0 0.2 pad_maximum_fusion.4
  93.5 0.5 convolution_convert_fusion
  94.2 0.7 reshape.197
  94.9 3.5 %all-to-all-start = ((bf16[4,2,1536]{2,1,0:T(2,128)(2,1)}), bf16[4,2,1536]{2,1,0:T(2,128)(2,1)S(1)}, u32[]{:S(2)}, u32[]{:S(2)}) async-start(bf16[4,2,1536]{2,1,0:T(2,128)(2,1)} %reshape.197), calls=%async_computation | async-start | bytes 49152 | tf_op jit(solution)/shard_map/all_to_all | solution.py:14
  98.5 3.6 %all-to-all-done = bf16[4,2,1536]{2,1,0:T(2,128)(2,1)S(1)} async-done(((bf16[4,2,1536]{2,1,0:T(2,128)(2,1)}), bf16[4,2,1536]{2,1,0:T(2,128)(2,1)S(1)}, u32[]{:S(2)}, u32[]{:S(2)}) %all-to-all-start) | async-done | bytes 24608 | tf_op jit(solution)/shard_map/all_to_all | solution.py:14
  102.2 0.2 copy.40
  102.4 1.1 %fusion = bf16[12,32,2,1280]{3,0,2,1:T(8,128)(2,1)S(1)} fusion(pred[32,1280]{1,0:T(8,128)(4,1)S(1)} %iota_compare_fusion, bf16[32,16,1280]{2,1,0:T(8,128)(2,1)S(1)} %copy-done, bf16[12,16,32,2]{0,3,2,1:T(2,128)(2,1)S(1)} %bitcast.199), kind=kOutput, calls=%fused_computation.1 | convolution fusion | flops 33423360 | bytes 3342336 | tf_op jit(solution)/shard_map/arqc,qrn->aqcn/dot_general | solution.py:83
  103.6 1.1 %copy.42 = bf16[12,32,2,1280]{3,1,2,0:T(8,128)(2,1)S(1)} copy(bf16[12,32,2,1280]{3,0,2,1:T(8,128)(2,1)S(1)} %fusion) | data formatting | bytes 3932160 | tf_op jit(solution)/shard_map/convert_element_type | solution.py:85
  104.6 3.3 %copy.43 = bf16[3,4,32,2,1280]{4,3,2,1,0:T(2,128)(2,1)} copy(bf16[3,4,32,2,1280]{4,2,3,1,0:T(8,128)(2,1)S(1)} %bitcast.198) | data formatting | bytes 3932160 | tf_op jit(solution)/shard_map/reshape | solution.py:86
  (36 shorter events, 0.8 us)
Async XLA Ops:
  0.0 102.4 %copy-start = (bf16[32,16,1280]{2,1,0:T(8,128)(2,1)S(1)}, bf16[32,16,1280]{2,1,0:T(8,128)(2,1)}, u32[]{:S(2)}) copy-start(bf16[32,16,1280]{2,1,0:T(8,128)(2,1)} %param.13) | copy-start | bytes 3932164
  2.2 15.3 %copy-start.11 = (s32[128]{0:T(128)S(1)}, s32[128]{0:T(128)}, u32[]{:S(2)}) copy-start(s32[128]{0:T(128)} %param.12) | copy-start | bytes 1540
  2.2 15.4 %copy-start.10 = (s32[4]{0:T(128)S(1)}, s32[4]{0:T(128)}, u32[]{:S(2)}) copy-start(s32[4]{0:T(128)} %param.9) | copy-start | bytes 52
  2.2 35.2 %collective-permute-start = (bf16[3,4,3,2688]{3,2,1,0:T(4,128)(2,1)}, bf16[3,4,3,2688]{3,2,1,0:T(4,128)(2,1)}, u32[]{:S(2)}, u32[]{:S(2)}) collective-permute-start(bf16[3,4,3,2688]{3,2,1,0:T(4,128)(2,1)} %get-tuple-element.16), channel_id=1, source_target_pairs={{0,8},{8,16},{16,24},{1,9},{9,17},{17,25},{2,10},{10,18},{18,26},{... | collective-permute-start | bytes 580616 | tf_op jit(solution)/shard_map/ppermute | solution.py:23
  4.8 32.7 %collective-permute-start.1 = (bf16[3,4,3,2688]{3,2,1,0:T(4,128)(2,1)}, bf16[3,4,3,2688]{3,2,1,0:T(4,128)(2,1)}, u32[]{:S(2)}, u32[]{:S(2)}) collective-permute-start(bf16[3,4,3,2688]{3,2,1,0:T(4,128)(2,1)} %get-tuple-element.17), channel_id=1, source_target_pairs={{8,0},{16,8},{24,16},{9,1},{17,9},{25,17},{10,2},{18,10},{26,18},{... | collective-permute-start | bytes 580616 | tf_op jit(solution)/shard_map/ppermute | solution.py:26
  23.3 2.5 %copy-start.1 = (f32[2688,128,1]{1,0,2:T(8,128)S(1)}, f32[2688,128,1]{1,0,2:T(8,128)}, u32[]{:S(2)}) copy-start(f32[2688,128,1]{1,0,2:T(8,128)} %get-tuple-element.23) | copy-start | bytes 4128772
  32.0 5.5 %copy-start.4 = (bf16[3,4,4,2688]{3,2,1,0:T(4,128)(2,1)S(1)}, bf16[3,4,4,2688]{3,2,1,0:T(4,128)(2,1)}, u32[]{:S(2)}) copy-start(bf16[3,4,4,2688]{3,2,1,0:T(4,128)(2,1)} %param.8) | copy-start | bytes 774148
  35.3 10.3 %copy-start.5 = (bf16[1,4,3,128,128]{4,3,2,1,0:T(8,128)(2,1)S(1)}, bf16[1,4,3,128,128]{4,3,2,1,0:T(8,128)(2,1)}, u32[]{:S(2)}) copy-start(bf16[1,4,3,128,128]{4,3,2,1,0:T(8,128)(2,1)} %get-tuple-element.9) | copy-start | bytes 1179652
  38.7 14.7 %collective-permute-start.2 = (bf16[3,1,10,2688]{3,2,1,0:T(8,128)(2,1)S(1)}, bf16[3,1,10,2688]{3,2,1,0:T(8,128)(2,1)S(1)}, u32[]{:S(2)}, u32[]{:S(2)}) collective-permute-start(bf16[3,1,10,2688]{3,2,1,0:T(8,128)(2,1)S(1)} %get-tuple-element.14), channel_id=1, source_target_pairs={{0,1},{1,2},{2,3},{3,4},{4,5},{5,6},{6,7},{8,9},{9,10},{10,11},{11... | collective-permute-start | bytes 483848 | tf_op jit(solution)/shard_map/ppermute | solution.py:23
  42.1 13.9 %collective-permute-start.3 = (bf16[3,1,10,2688]{3,2,1,0:T(8,128)(2,1)S(1)}, bf16[3,1,10,2688]{3,2,1,0:T(8,128)(2,1)S(1)}, u32[]{:S(2)}, u32[]{:S(2)}) collective-permute-start(bf16[3,1,10,2688]{3,2,1,0:T(8,128)(2,1)S(1)} %get-tuple-element.15), channel_id=1, source_target_pairs={{1,0},{2,1},{3,2},{4,3},{5,4},{6,5},{7,6},{9,8},{10,9},{11,10},{12... | collective-permute-start | bytes 483848 | tf_op jit(solution)/shard_map/ppermute | solution.py:26
  62.1 6.1 %copy-start.6 = (bf16[4,3,128,128]{3,2,0,1:T(8,128)(2,1)S(1)}, bf16[4,3,128,128]{3,2,0,1:T(8,128)(2,1)}, u32[]{:S(2)}) copy-start(bf16[4,3,128,128]{3,2,0,1:T(8,128)(2,1)} %get-tuple-element.39) | copy-start | bytes 1179652
  63.3 3.7 %copy-start.2 = (bf16[3,6,4,21,128]{4,3,2,1,0:T(8,128)(2,1)}, bf16[3,6,4,21,128]{4,3,2,1,0:T(8,128)(2,1)S(1)}, u32[]{:S(2)}) copy-start(bf16[3,6,4,21,128]{4,3,2,1,0:T(8,128)(2,1)S(1)} %reshape.166) | copy-start | bytes 1161220
  68.2 1.8 %copy-start.7 = (bf16[3,6,4,2688]{3,2,1,0:T(4,128)(2,1)S(1)}, bf16[3,6,4,2688]{3,2,1,0:T(4,128)(2,1)}, u32[]{:S(2)}) copy-start(bf16[3,6,4,2688]{3,2,1,0:T(4,128)(2,1)} %get-tuple-element.11) | copy-start | bytes 1161220
  68.2 1.8 %copy-start.8 = (bf16[3,6,4,2688]{3,2,1,0:T(4,128)(2,1)S(1)}, bf16[3,6,4,2688]{3,2,1,0:T(4,128)(2,1)}, u32[]{:S(2)}) copy-start(bf16[3,6,4,2688]{3,2,1,0:T(4,128)(2,1)} %get-tuple-element.12) | copy-start | bytes 1161220
  80.1 3.8 %copy-start.3 = (bf16[3,6,4,21,128]{4,3,2,1,0:T(8,128)(2,1)S(1)}, bf16[3,6,4,21,128]{4,3,2,1,0:T(8,128)(2,1)}, u32[]{:S(2)}) copy-start(bf16[3,6,4,21,128]{4,3,2,1,0:T(8,128)(2,1)} %copy-done.2) | copy-start | bytes 1161220
  89.2 3.8 %copy-start.9 = (bf16[3,4,1,2688]{3,1,0,2:T(4,128)(2,1)S(1)}, bf16[3,4,1,2688]{3,1,0,2:T(4,128)(2,1)}, u32[]{:S(2)}) copy-start(bf16[3,4,1,2688]{3,1,0,2:T(4,128)(2,1)} %stack_reshape.17) | copy-start | bytes 193540
  94.9 7.2 %all-to-all-start = ((bf16[4,2,1536]{2,1,0:T(2,128)(2,1)}), bf16[4,2,1536]{2,1,0:T(2,128)(2,1)S(1)}, u32[]{:S(2)}, u32[]{:S(2)}) async-start(bf16[4,2,1536]{2,1,0:T(2,128)(2,1)} %reshape.197), calls=%async_computation | async-start | bytes 49152 | tf_op jit(solution)/shard_map/all_to_all | solution.py:14
